TPU v7x, 512 devices: a whole 4x4x16 slice. The times are simulated.
512 devices in a mesh: grp: 64 (over z, x_lo, core), rep: 8 (over y, x_hi).
Axes of the slice: x: 4 (x_hi: 2, x_lo: 2; x = x_hi * 2 + x_lo), y: 4, z: 16, core: 2. Of those that a mesh axis runs over, the one named last changes fastest.
Arguments:
- adjoint: bfloat16 [1024, 512], P('grp'), may hold values from -6 to 6
- active: int32 [1024, 512], P('grp'), may hold values 0 or 1
- counts: int32 [1024, 65536], P('rep', 'grp'), may hold values from 0 to 3, as said below
- src_degree: int32 [1024], P('rep'), may hold values from 8 to 256
- dst_degree: int32 [65536], P('grp'), may hold values from 8 to 256
- inputs: bfloat16 [65536, 512], P(('grp', 'rep')), may hold values from -6 to 6
- weight: bfloat16 [512, 512], replicated, may hold values from -0.25 to 0.25
Outputs:
- grad_input: bfloat16 [65536, 512], P(('grp', 'rep'))
- grad_weight: float32 [512, 512], P('rep')
Inputs may be any that keep to these rules, and one draw needn't show every extreme that they name: Edge counts; within an aligned tile of 16 source rows by 1024 destination columns the share of nonzero entries ranges from none to all, differing from tile to tile.
All inputs are finite; a program needn't handle non-finite values. No bound on the sum of `active` on one device may be relied on, other than what follows from the above.
Results may differ from a plain program's by a relative error of at most 0.0057.
Values may be sent and summed in bfloat16 or wider, within the bound.
A program may use at most 64 MiB of HBM per device.

v0:
```python
import jax
import jax.numpy as jnp
from jax import lax
from jax.sharding import PartitionSpec as P


def spread(shard, axis, root):
    mine = lax.axis_index(axis) == root
    return lax.psum(jnp.where(mine, shard, jnp.zeros_like(shard)), axis)


def weight_term(row_inputs, values):
    high_part = values.astype(jnp.bfloat16)
    low_part = (values - high_part.astype(jnp.float32)).astype(jnp.bfloat16)
    upper = lax.dot_general(
        row_inputs, high_part, (((0,), (0,)), ((), ())), preferred_element_type=jnp.float32
    )
    lower = lax.dot_general(
        row_inputs, low_part, (((0,), (0,)), ((), ())), preferred_element_type=jnp.float32
    )
    return upper + lower


def body(adjoint, active, counts, src_degree, dst_degree, inputs, weight):
    masked = (adjoint.astype(jnp.float32) * active.astype(jnp.float32)).astype(jnp.bfloat16)
    src_scale = lax.rsqrt(src_degree.astype(jnp.float32))
    dst_scale = lax.rsqrt(dst_degree.astype(jnp.float32))
    src_rows = adjoint.shape[0]
    blocks = counts.shape[0] // src_rows
    replica = lax.axis_index("rep")

    def scaled_product(count_tile, row_scale, owner_rows, running):
        scaled_tile = (
            count_tile.astype(jnp.float32) * row_scale[:, None] * dst_scale[None, :]
        ).astype(jnp.bfloat16)
        return running + lax.dot_general(
            scaled_tile, owner_rows, (((0,), (0,)), ((), ())), preferred_element_type=jnp.float32
        )

    def apply_tile(block_index, running):
        owner_index = replica * blocks + block_index
        owner_rows = spread(masked, "grp", owner_index)
        start = block_index * src_rows
        count_tile = lax.dynamic_slice_in_dim(counts, start, src_rows, 0)
        row_scale = lax.dynamic_slice_in_dim(src_scale, start, src_rows, 0)
        return scaled_product(count_tile, row_scale, owner_rows, running)

    partial_value = lax.fori_loop(
        0, blocks, apply_tile, jnp.zeros((counts.shape[1], masked.shape[1]), jnp.float32)
    )
    grad_pre = lax.psum_scatter(partial_value, "rep", scatter_dimension=0, tiled=True)
    grad_input = lax.dot_general(
        grad_pre.astype(jnp.bfloat16),
        weight,
        (((1,), (1,)), ((), ())),
        preferred_element_type=jnp.float32,
    ).astype(jnp.bfloat16)
    vertex_total = inputs.shape[0] * lax.axis_size("grp") * lax.axis_size("rep")
    local_term = weight_term(inputs, grad_pre)
    whole_term = lax.psum(local_term, "grp")
    grad_weight = lax.psum_scatter(whole_term, "rep", scatter_dimension=0, tiled=True)
    return (grad_input, grad_weight / vertex_total)


def solution(mesh):
    in_specs = (
        P("grp", None),
        P("grp", None),
        P("rep", "grp"),
        P("rep"),
        P("grp"),
        P(("grp", "rep"), None),
        P(),
    )
    out_specs = (P(("grp", "rep"), None), P("rep", None))
    return jax.shard_map(body, mesh=mesh, in_specs=in_specs, out_specs=out_specs, check_vma=False)
```

profile of v0, /device:TPU:1, one launch (start us, length us, event | category | flops | bytes accessed | tf_op | source)
XLA Modules:
  0.0 2293.0 jit_solution(14087357009032355527)
XLA Ops:
  7.2 0.0 copy-start
  7.2 0.0 reduce-scatter.5.cloned.1.call-start
  7.2 0.7 convert_rsqrt_fusion.1
  7.9 0.7 convert_rsqrt_fusion
  8.6 0.8 multiply_convert_fusion.2
  9.4 1680.2 %while.16 = (s32[]{:T(128)}, f32[1024,512]{1,0:T(8,128)S(1)}, s32[128,1024]{1,0:T(8,128)}, f32[128]{0:T(128)S(1)}, f32[1024]{0:T(1024)S(1)}, /*index=5*/s32[]{:T...) while((s32[]{:T(128)}, f32[1024,512]{1,0:T(8,128)S(1)}, ...), condition=%wide.region_2.3_spmd.clone, body=%wide.region_0.2_spmd.clone.sunk | while | flops 17907724 | bytes 4346299 | solution.py:48
  9.4 0.1 dynamic_slice.25
  9.5 214.4 %psum.24 = bf16[16,512]{1,0:T(8,128)(2,1)S(1)} all-reduce(bf16[16,512]{1,0:T(8,128)(2,1)S(1)} %broadcast_select_fusion.2), channel_id=1, replica_groups=mesh['grp'=64,'rep'=8] {'grp'}, use_global_device_ids=true, to_apply=%region_1.1 | all-reduce | flops 8192 | bytes 32768 | tf_op jit(solution)/shard_map/while/body/eval_jaxpr/psum | solution.py:9
  223.9 1.6 select_add_fusion.2
  225.5 0.1 dynamic_slice.25
  225.6 207.5 %psum.24 = bf16[16,512]{1,0:T(8,128)(2,1)S(1)} all-reduce(bf16[16,512]{1,0:T(8,128)(2,1)S(1)} %broadcast_select_fusion.2), channel_id=1, replica_groups=mesh['grp'=64,'rep'=8] {'grp'}, use_global_device_ids=true, to_apply=%region_1.1 | all-reduce | flops 8192 | bytes 32768 | tf_op jit(solution)/shard_map/while/body/eval_jaxpr/psum | solution.py:9
  433.1 1.5 select_add_fusion.2
  434.6 0.1 dynamic_slice.25
  434.7 207.5 %psum.24 = bf16[16,512]{1,0:T(8,128)(2,1)S(1)} all-reduce(bf16[16,512]{1,0:T(8,128)(2,1)S(1)} %broadcast_select_fusion.2), channel_id=1, replica_groups=mesh['grp'=64,'rep'=8] {'grp'}, use_global_device_ids=true, to_apply=%region_1.1 | all-reduce | flops 8192 | bytes 32768 | tf_op jit(solution)/shard_map/while/body/eval_jaxpr/psum | solution.py:9
  642.2 1.6 select_add_fusion.2
  643.8 0.1 dynamic_slice.25
  643.9 207.5 %psum.24 = bf16[16,512]{1,0:T(8,128)(2,1)S(1)} all-reduce(bf16[16,512]{1,0:T(8,128)(2,1)S(1)} %broadcast_select_fusion.2), channel_id=1, replica_groups=mesh['grp'=64,'rep'=8] {'grp'}, use_global_device_ids=true, to_apply=%region_1.1 | all-reduce | flops 8192 | bytes 32768 | tf_op jit(solution)/shard_map/while/body/eval_jaxpr/psum | solution.py:9
  851.4 1.5 select_add_fusion.2
  853.0 0.1 dynamic_slice.25
  853.1 207.5 %psum.24 = bf16[16,512]{1,0:T(8,128)(2,1)S(1)} all-reduce(bf16[16,512]{1,0:T(8,128)(2,1)S(1)} %broadcast_select_fusion.2), channel_id=1, replica_groups=mesh['grp'=64,'rep'=8] {'grp'}, use_global_device_ids=true, to_apply=%region_1.1 | all-reduce | flops 8192 | bytes 32768 | tf_op jit(solution)/shard_map/while/body/eval_jaxpr/psum | solution.py:9
  1060.6 1.6 select_add_fusion.2
  1062.2 0.1 dynamic_slice.25
  1062.2 207.5 %psum.24 = bf16[16,512]{1,0:T(8,128)(2,1)S(1)} all-reduce(bf16[16,512]{1,0:T(8,128)(2,1)S(1)} %broadcast_select_fusion.2), channel_id=1, replica_groups=mesh['grp'=64,'rep'=8] {'grp'}, use_global_device_ids=true, to_apply=%region_1.1 | all-reduce | flops 8192 | bytes 32768 | tf_op jit(solution)/shard_map/while/body/eval_jaxpr/psum | solution.py:9
  1269.7 1.5 select_add_fusion.2
  1271.3 0.1 dynamic_slice.25
  1271.4 207.5 %psum.24 = bf16[16,512]{1,0:T(8,128)(2,1)S(1)} all-reduce(bf16[16,512]{1,0:T(8,128)(2,1)S(1)} %broadcast_select_fusion.2), channel_id=1, replica_groups=mesh['grp'=64,'rep'=8] {'grp'}, use_global_device_ids=true, to_apply=%region_1.1 | all-reduce | flops 8192 | bytes 32768 | tf_op jit(solution)/shard_map/while/body/eval_jaxpr/psum | solution.py:9
  1478.9 1.6 select_add_fusion.2
  1480.5 0.1 dynamic_slice.25
  1480.6 207.5 %psum.24 = bf16[16,512]{1,0:T(8,128)(2,1)S(1)} all-reduce(bf16[16,512]{1,0:T(8,128)(2,1)S(1)} %broadcast_select_fusion.2), channel_id=1, replica_groups=mesh['grp'=64,'rep'=8] {'grp'}, use_global_device_ids=true, to_apply=%region_1.1 | all-reduce | flops 8192 | bytes 32768 | tf_op jit(solution)/shard_map/while/body/eval_jaxpr/psum | solution.py:9
  1688.1 1.5 select_add_fusion.2
  1689.6 0.0 copy-start.1
  1689.7 0.0 copy-start.3
  1689.7 1.3 copy-done.1
  1691.0 0.0 reduce-scatter.5.cloned.1.call-update
  1691.0 0.0 reduce-scatter.7.cloned.1.call-start
  1691.1 89.1 %reduce-scatter.5.cloned.1.call-done = f32[128,512]{1,0:T(8,128)} async-done(((f32[1024,512]{1,0:T(8,128)}), f32[128,512]{1,0:T(8,128)}) %reduce-scatter.5.cloned.1.call-update) | async-done | bytes 262160 | tf_op jit(solution)/shard_map/reduce_scatter | solution.py:51
  1780.1 0.0 copy-done.3
  1780.1 1.3 fusion.5
  1781.4 1.4 fusion.3
  1782.7 0.0 copy-start.2
  1782.8 1.3 copy.11
  1784.1 0.0 reduce-scatter.7.cloned.1.call-update
  1784.1 0.0 all-reduce.2.cloned.1.call-start
  1784.1 86.7 %reduce-scatter.7.cloned.1.call-done = f32[64,512]{1,0:T(8,128)} async-done(((f32[512,512]{1,0:T(8,128)}), f32[64,512]{1,0:T(8,128)}) %reduce-scatter.7.cloned.1.call-update) | async-done | bytes 131088
  1870.9 1.7 copy.12
  1872.6 0.0 all-reduce.2.cloned.1.call-update
  1872.6 0.0 copy-done
  1872.6 0.0 copy-done.2
  1872.6 1.0 convolution_convert_fusion
  1873.6 411.2 %all-reduce.2.cloned.1.call-done = f32[64,512]{0,1:T(8,128)} async-done(((f32[64,512]{0,1:T(8,128)}), f32[64,512]{0,1:T(8,128)}) %all-reduce.2.cloned.1.call-update) | async-done | bytes 131088 | tf_op jit(solution)/shard_map/psum | solution.py:60
  2284.8 1.0 broadcast_multiply_fusion
  2285.7 0.8 copy.10
  (9 shorter events, 0.1 us)
Async XLA Ops:
  7.2 1865.5 %copy-start = (bf16[512,512]{1,0:T(8,128)(2,1)S(1)}, bf16[512,512]{1,0:T(8,128)(2,1)}, u32[]{:S(2)}) copy-start(bf16[512,512]{1,0:T(8,128)(2,1)} %param.15) | copy-start | bytes 1572868
  7.2 1772.9 %reduce-scatter.5.cloned.1.call-start = ((), (), s32[]{:S(2)}) async-start(), calls=%async_computation.2 | async-start | bytes 2359296 | tf_op jit(solution)/shard_map/reduce_scatter | solution.py:51
  1689.6 1.3 copy-start.1
  1689.7 90.5 %copy-start.3 = (bf16[128,512]{1,0:T(8,128)(2,1)S(1)}, bf16[128,512]{1,0:T(8,128)(2,1)}, u32[]{:S(2)}) copy-start(bf16[128,512]{1,0:T(8,128)(2,1)} %param.14) | copy-start | bytes 393220
  1691.0 179.9 %reduce-scatter.7.cloned.1.call-start = ((), (), s32[]{:S(2)}) async-start(), calls=%async_computation.4 | async-start | bytes 1179648
  1782.7 89.9 %copy-start.2 = (f32[128,512]{1,0:T(8,128)S(1)}, f32[128,512]{1,0:T(8,128)}, u32[]{:S(2)}) copy-start(f32[128,512]{1,0:T(8,128)} %reduce-scatter.5.cloned.1.call-done) | copy-start | bytes 786436
  1784.1 500.7 %all-reduce.2.cloned.1.call-start = ((), (), s32[]{:S(2)}) async-start(), calls=%async_computation.3 | async-start | bytes 524288 | tf_op jit(solution)/shard_map/psum | solution.py:60
Sparse Core Ops, SparseCore 0:
  1691.1 88.9 reduce-scatter.4
  1784.6 86.2 reduce-scatter.6
  1873.8 410.9 all-reduce.1
where the time goes:
time: 2290 us
  blocking collectives  1670 us (73%)
  waiting for transfers between devices  587 us (26%)
    psum x8, blocking collectives, spread(): return lax.psum(jnp.where(mine, shard, jnp.zeros_like(shard)), axis)  1670 us
    psum x1, waiting for transfers between devices, body(): whole_term = lax.psum(local_term, 'grp')  411 us
    reduce_scatter x1, waiting for transfers between devices, body(): lax.psum_scatter(partial_value, 'rep', scatter_dimension=0, tiled=True)  89.1 us
    unnamed x4, waiting for transfers between devices  86.8 us
  transfers between devices with their start and end apart: 3, of which 3 were waited for; matrix products, arithmetic and copies ran while one was open for 0% of the time, Pallas kernels for 0%

commit v1 on v0

--- a/solution.py
+++ b/solution.py
@@ -6,7 +6,10 @@
 
 def spread(shard, axis, root):
     mine = lax.axis_index(axis) == root
-    return lax.psum(jnp.where(mine, shard, jnp.zeros_like(shard)), axis)
+    refer_quotas = lambda local_block, which_axis: jnp.sum(
+        lax.all_gather(local_block, which_axis), axis=0
+    )
+    return refer_quotas(jnp.where(mine, shard, jnp.zeros_like(shard)), axis)
 
 
 def weight_term(row_inputs, values):

time: 2290 us -> 1620 us (0.71)
  blocking collectives: 1670 us -> 0 us
  waiting for transfers between devices: 587 us -> 1560 us
    psum x8 -> x0, blocking collectives: 1670 us -> none  [spread(): return lax.psum(jnp.where(mine, shard, jnp.zeros_like(shard)), axis)]
    all_gather x0 -> x8, waiting for transfers between devices: none -> 972 us  [spread(): lax.all_gather(local_block, which_axis)]
  transfers between devices with their start and end apart: 3 -> 11, of which waited for: 3 -> 11; matrix products, arithmetic and copies ran while one was open for 0% -> 0% of each run, Pallas kernels for 0% -> 0%
where the time goes in v1:
time: 1620 us
  waiting for transfers between devices  1560 us (96%)
  other arithmetic  19.3 us (1%)
    all_gather x8, waiting for transfers between devices, spread(): lax.all_gather(local_block, which_axis)  972 us
    psum x1, waiting for transfers between devices, body(): whole_term = lax.psum(local_term, 'grp')  411 us
    reduce_scatter x1, waiting for transfers between devices, body(): lax.psum_scatter(partial_value, 'rep', scatter_dimension=0, tiled=True)  89.9 us
    unnamed x4, waiting for transfers between devices  86.8 us
  transfers between devices with their start and end apart: 11, of which 11 were waited for; matrix products, arithmetic and copies ran while one was open for 0% of the time, Pallas kernels for 0%

profile of v1, /device:TPU:1, one launch (start us, length us, event | category | flops | bytes accessed | tf_op | source)
XLA Modules:
  0.0 1617.9 jit_solution(11650293335633039890)
XLA Ops:
  8.0 0.7 convert_rsqrt_fusion.1
  8.7 0.7 convert_rsqrt_fusion
  9.4 0.8 multiply_convert_fusion.2
  10.2 1002.1 %while.16 = (s32[]{:T(128)}, f32[1024,512]{1,0:T(8,128)S(1)}, s32[128,1024]{1,0:T(8,128)}, f32[128]{0:T(128)S(1)}, f32[1024]{0:T(1024)S(1)}, /*index=5*/s32[]{:T...) while((s32[]{:T(128)}, f32[1024,512]{1,0:T(8,128)S(1)}, ...), condition=%wide.region_2.3_spmd.clone, body=%wide.region_0.2_spmd.clone.sunk | while | flops 18415628 | bytes 8573421 | solution.py:51
  10.2 0.0 all-gather.6.cloned.1.call-start
  10.3 0.6 broadcast_select_fusion.2
  10.9 0.1 all-gather.6.cloned.1.call-update
  11.0 0.1 dynamic_slice.27
  11.0 129.6 %all-gather.6.cloned.1.call-done = bf16[1024,512]{1,0:T(8,128)(2,1)} async-done(((bf16[16,512]{1,0:T(8,128)(2,1)}), bf16[1024,512]{1,0:T(8,128)(2,1)}) %all-gather.6.cloned.1.call-update) | async-done | bytes 1048592 | tf_op jit(solution)/shard_map/while/body/eval_jaxpr/all_gather | solution.py:10
  140.6 1.4 reduce_sum.16
  142.0 1.6 select_add_fusion.2
  143.7 0.6 broadcast_select_fusion.2
  144.3 0.1 all-gather.6.cloned.1.call-update
  144.4 0.1 dynamic_slice.27
  144.4 120.4 %all-gather.6.cloned.1.call-done = bf16[1024,512]{1,0:T(8,128)(2,1)} async-done(((bf16[16,512]{1,0:T(8,128)(2,1)}), bf16[1024,512]{1,0:T(8,128)(2,1)}) %all-gather.6.cloned.1.call-update) | async-done | bytes 1048592 | tf_op jit(solution)/shard_map/while/body/eval_jaxpr/all_gather | solution.py:10
  264.9 1.4 reduce_sum.16
  266.3 1.6 select_add_fusion.2
  267.9 0.6 broadcast_select_fusion.2
  268.5 0.1 all-gather.6.cloned.1.call-update
  268.6 0.1 dynamic_slice.27
  268.7 120.4 %all-gather.6.cloned.1.call-done = bf16[1024,512]{1,0:T(8,128)(2,1)} async-done(((bf16[16,512]{1,0:T(8,128)(2,1)}), bf16[1024,512]{1,0:T(8,128)(2,1)}) %all-gather.6.cloned.1.call-update) | async-done | bytes 1048592 | tf_op jit(solution)/shard_map/while/body/eval_jaxpr/all_gather | solution.py:10
  389.1 1.4 reduce_sum.16
  390.5 1.6 select_add_fusion.2
  392.1 0.6 broadcast_select_fusion.2
  392.8 0.1 dynamic_slice.27
  392.8 120.2 %all-gather.6.cloned.1.call-done = bf16[1024,512]{1,0:T(8,128)(2,1)} async-done(((bf16[16,512]{1,0:T(8,128)(2,1)}), bf16[1024,512]{1,0:T(8,128)(2,1)}) %all-gather.6.cloned.1.call-update) | async-done | bytes 1048592 | tf_op jit(solution)/shard_map/while/body/eval_jaxpr/all_gather | solution.py:10
  513.0 1.4 reduce_sum.16
  514.4 1.6 select_add_fusion.2
  516.0 0.6 broadcast_select_fusion.2
  516.7 0.1 dynamic_slice.27
  516.8 120.2 %all-gather.6.cloned.1.call-done = bf16[1024,512]{1,0:T(8,128)(2,1)} async-done(((bf16[16,512]{1,0:T(8,128)(2,1)}), bf16[1024,512]{1,0:T(8,128)(2,1)}) %all-gather.6.cloned.1.call-update) | async-done | bytes 1048592 | tf_op jit(solution)/shard_map/while/body/eval_jaxpr/all_gather | solution.py:10
  636.9 1.4 reduce_sum.16
  638.3 1.6 select_add_fusion.2
  640.0 0.6 broadcast_select_fusion.2
  640.6 0.1 dynamic_slice.27
  640.7 120.2 %all-gather.6.cloned.1.call-done = bf16[1024,512]{1,0:T(8,128)(2,1)} async-done(((bf16[16,512]{1,0:T(8,128)(2,1)}), bf16[1024,512]{1,0:T(8,128)(2,1)}) %all-gather.6.cloned.1.call-update) | async-done | bytes 1048592 | tf_op jit(solution)/shard_map/while/body/eval_jaxpr/all_gather | solution.py:10
  760.8 1.4 reduce_sum.16
  762.2 1.6 select_add_fusion.2
  763.9 0.6 broadcast_select_fusion.2
  764.5 0.1 all-gather.6.cloned.1.call-update
  764.6 0.1 dynamic_slice.27
  764.7 120.4 %all-gather.6.cloned.1.call-done = bf16[1024,512]{1,0:T(8,128)(2,1)} async-done(((bf16[16,512]{1,0:T(8,128)(2,1)}), bf16[1024,512]{1,0:T(8,128)(2,1)}) %all-gather.6.cloned.1.call-update) | async-done | bytes 1048592 | tf_op jit(solution)/shard_map/while/body/eval_jaxpr/all_gather | solution.py:10
  885.1 1.4 reduce_sum.16
  886.5 1.6 select_add_fusion.2
  888.1 0.6 broadcast_select_fusion.2
  888.7 0.1 all-gather.6.cloned.1.call-update
  888.8 0.1 dynamic_slice.27
  888.9 120.4 %all-gather.6.cloned.1.call-done = bf16[1024,512]{1,0:T(8,128)(2,1)} async-done(((bf16[16,512]{1,0:T(8,128)(2,1)}), bf16[1024,512]{1,0:T(8,128)(2,1)}) %all-gather.6.cloned.1.call-update) | async-done | bytes 1048592 | tf_op jit(solution)/shard_map/while/body/eval_jaxpr/all_gather | solution.py:10
  1009.3 1.4 reduce_sum.16
  1010.7 1.6 select_add_fusion.2
  1012.3 0.0 reduce-scatter.5.cloned.1.call-start
  1012.4 1.3 copy-done.1
  1013.7 0.0 reduce-scatter.7.cloned.1.call-start
  1013.7 89.9 %reduce-scatter.5.cloned.1.call-done = f32[128,512]{1,0:T(8,128)} async-done(((f32[1024,512]{1,0:T(8,128)}), f32[128,512]{1,0:T(8,128)}) %reduce-scatter.5.cloned.1.call-update) | async-done | bytes 262160 | tf_op jit(solution)/shard_map/reduce_scatter | solution.py:54
  1103.6 1.3 fusion.5
  1104.8 1.3 fusion.3
  1106.2 1.3 copy.11
  1107.5 0.0 all-reduce.2.cloned.1.call-start
  1107.6 86.7 %reduce-scatter.7.cloned.1.call-done = f32[64,512]{1,0:T(8,128)} async-done(((f32[512,512]{1,0:T(8,128)}), f32[64,512]{1,0:T(8,128)}) %reduce-scatter.7.cloned.1.call-update) | async-done | bytes 131088
  1194.3 1.7 copy.12
  1196.1 1.0 convolution_convert_fusion
  1197.1 411.5 %all-reduce.2.cloned.1.call-done = f32[64,512]{0,1:T(8,128)} async-done(((f32[64,512]{0,1:T(8,128)}), f32[64,512]{0,1:T(8,128)}) %all-reduce.2.cloned.1.call-update) | async-done | bytes 131088 | tf_op jit(solution)/shard_map/psum | solution.py:63
  1608.5 1.0 broadcast_multiply_fusion
  1609.5 0.8 copy.10
  (21 shorter events, 0.4 us)
Async XLA Ops:
  8.0 1188.1 %copy-start = (bf16[512,512]{1,0:T(8,128)(2,1)S(1)}, bf16[512,512]{1,0:T(8,128)(2,1)}, u32[]{:S(2)}) copy-start(bf16[512,512]{1,0:T(8,128)(2,1)} %param.15) | copy-start | bytes 1572868
  10.2 130.4 %all-gather.6.cloned.1.call-start = ((), (), s32[]{:S(2)}) async-start(), calls=%async_computation.5 | async-start | bytes 1064960 | tf_op jit(solution)/shard_map/while/body/eval_jaxpr/all_gather | solution.py:10
  143.6 121.3 %all-gather.6.cloned.1.call-start = ((), (), s32[]{:S(2)}) async-start(), calls=%async_computation.5 | async-start | bytes 1064960 | tf_op jit(solution)/shard_map/while/body/eval_jaxpr/all_gather | solution.py:10
  267.8 121.2 %all-gather.6.cloned.1.call-start = ((), (), s32[]{:S(2)}) async-start(), calls=%async_computation.5 | async-start | bytes 1064960 | tf_op jit(solution)/shard_map/while/body/eval_jaxpr/all_gather | solution.py:10
  392.1 120.9 %all-gather.6.cloned.1.call-start = ((), (), s32[]{:S(2)}) async-start(), calls=%async_computation.5 | async-start | bytes 1064960 | tf_op jit(solution)/shard_map/while/body/eval_jaxpr/all_gather | solution.py:10
  516.0 120.9 %all-gather.6.cloned.1.call-start = ((), (), s32[]{:S(2)}) async-start(), calls=%async_computation.5 | async-start | bytes 1064960 | tf_op jit(solution)/shard_map/while/body/eval_jaxpr/all_gather | solution.py:10
  639.9 120.9 %all-gather.6.cloned.1.call-start = ((), (), s32[]{:S(2)}) async-start(), calls=%async_computation.5 | async-start | bytes 1064960 | tf_op jit(solution)/shard_map/while/body/eval_jaxpr/all_gather | solution.py:10
  763.8 121.3 %all-gather.6.cloned.1.call-start = ((), (), s32[]{:S(2)}) async-start(), calls=%async_computation.5 | async-start | bytes 1064960 | tf_op jit(solution)/shard_map/while/body/eval_jaxpr/all_gather | solution.py:10
  888.1 121.3 %all-gather.6.cloned.1.call-start = ((), (), s32[]{:S(2)}) async-start(), calls=%async_computation.5 | async-start | bytes 1064960 | tf_op jit(solution)/shard_map/while/body/eval_jaxpr/all_gather | solution.py:10
  1012.3 1.3 copy-start.1
  1012.3 91.3 %copy-start.3 = (bf16[128,512]{1,0:T(8,128)(2,1)S(1)}, bf16[128,512]{1,0:T(8,128)(2,1)}, u32[]{:S(2)}) copy-start(bf16[128,512]{1,0:T(8,128)(2,1)} %param.14) | copy-start | bytes 393220
  1012.3 91.3 %reduce-scatter.5.cloned.1.call-start = ((), (), s32[]{:S(2)}) async-start(), calls=%async_computation.2 | async-start | bytes 2359296 | tf_op jit(solution)/shard_map/reduce_scatter | solution.py:54
  1013.7 180.7 %reduce-scatter.7.cloned.1.call-start = ((), (), s32[]{:S(2)}) async-start(), calls=%async_computation.4 | async-start | bytes 1179648
  1106.2 89.9 %copy-start.2 = (f32[128,512]{1,0:T(8,128)S(1)}, f32[128,512]{1,0:T(8,128)}, u32[]{:S(2)}) copy-start(f32[128,512]{1,0:T(8,128)} %reduce-scatter.5.cloned.1.call-done) | copy-start | bytes 786436
  1107.5 501.0 %all-reduce.2.cloned.1.call-start = ((), (), s32[]{:S(2)}) async-start(), calls=%async_computation.3 | async-start | bytes 524288 | tf_op jit(solution)/shard_map/psum | solution.py:63
Sparse Core Ops, SparseCore 0:
  13.8 126.8 all-gather.5
  147.1 117.6 all-gather.5
  271.4 117.6 all-gather.5
  395.3 117.6 all-gather.5
  519.2 117.6 all-gather.5
  643.1 117.6 all-gather.5
  767.4 117.6 all-gather.5
  891.6 117.6 all-gather.5
Sparse Core Ops, SparseCore 1:
  1017.4 86.1 reduce-scatter.4
  1107.9 86.4 reduce-scatter.6
  1197.1 411.4 all-reduce.1
